TPU v7x, 512 devices: a whole 4x8x8 slice. The times are simulated.
512 devices in a mesh: dp: 32 (over y, x), col: 16 (over z, core).
Axes of the slice: x: 4, y: 8, z: 8, core: 2. Of those that a mesh axis runs over, the one named last changes fastest.
Arguments:
- grad_out: bfloat16 [32768, 3584], P('dp', 'col'), may hold values from -6 to 6
- residual: bfloat16 [32768, 3584], P('dp', 'col'), may hold values from -6 to 6
- confounders: bfloat16 [32768, 512], P('dp'), may hold values from -6 to 6
- gram_factor: float32 [512, 512], replicated, as said below
- proj_weight: bfloat16 [3584, 3584], P('dp', 'col'), may hold values from -0.09375 to 0.09375
- doc_lengths: int32 [32768], P(('dp', 'col')), may hold values from 1 to 512, as said below
Outputs:
- token_grad: float32 [32768, 3584], P(('dp', 'col'))
- weight_grad: float32 [3584, 3584], P('dp', 'col')
Inputs may be any that keep to these rules, and one draw needn't show every extreme that they name: `gram_factor`: lower triangular with a positive diagonal. `doc_lengths`: at least one document has 512 tokens.
All inputs are finite; a program needn't handle non-finite values.
Results may differ from a plain program's by a relative error of at most 0.0026.
Values may be sent and summed in bfloat16 or wider, within the bound.
No kernel may reach another device: no remote copies, remote signals or barrier semaphores. Data moves between devices by JAX's collectives and lax.ppermute only.
A program may use at most 64 MiB of HBM per device.

v0:
```python
import jax
import jax.numpy as jnp
from jax import lax
from jax.sharding import PartitionSpec as P


def solve_gram(factor, rhs):
    inner = lax.linalg.triangular_solve(factor, rhs, left_side=True, lower=True)
    return lax.linalg.triangular_solve(factor, inner, left_side=True, lower=True, transpose_a=True)


def shards(grad_out, residual, confounders, gram_factor, proj_weight, doc_lengths):
    grad_full = lax.all_gather(grad_out, "col", axis=1, tiled=True)
    docs_total = grad_out.shape[0] * lax.axis_size("dp")
    norm_scale = docs_total ** (-0.5)
    own_rows = proj_weight.shape[0]
    full_term = lax.dot_general(
        grad_full, residual, (((0,), (0,)), ((), ())), preferred_element_type=jnp.float32
    )
    summed_all = lax.psum(full_term, "dp")
    summed = lax.dynamic_slice_in_dim(summed_all, lax.axis_index("dp") * own_rows, own_rows, 0)
    weight_grad = summed * norm_scale
    dense_grad = jnp.dot(
        grad_full,
        lax.all_gather(proj_weight, "dp", axis=0, tiled=True),
        preferred_element_type=jnp.float32,
    )
    dense_b = dense_grad.astype(jnp.bfloat16)
    partial_value = lax.dot_general(
        confounders, dense_b, (((0,), (0,)), ((), ())), preferred_element_type=jnp.float32
    )
    moments = lax.psum(partial_value, "dp")
    coef_b = solve_gram(gram_factor, moments).astype(jnp.bfloat16)
    pooled = dense_grad - jnp.dot(confounders, coef_b, preferred_element_type=jnp.float32)
    doc_grad = lax.all_to_all(pooled, "col", split_axis=0, concat_axis=1, tiled=True)
    token_grad = doc_grad / doc_lengths.astype(jnp.float32)[:, None]
    return (token_grad, weight_grad)


def solution(mesh):
    placed = (P("dp", "col"), P("dp", "col"), P("dp", None), P(), P("dp", "col"), P(("dp", "col")))
    return jax.shard_map(
        shards,
        mesh=mesh,
        in_specs=placed,
        out_specs=(P(("dp", "col"), None), P("dp", "col")),
        check_vma=False,
    )
```

profile of v0, /device:TPU:1, one launch (start us, length us, event | category | flops | bytes accessed | tf_op | source)
XLA Modules:
  0.0 392.3 jit_solution(9254413336297546510)
XLA Ops:
  7.2 0.0 all-gather.5.cloned.1.call-start
  7.2 0.7 all-gather.5.cloned.1.call-update
  7.9 0.0 all-gather.3.cloned.1.call-start
  8.0 0.7 all-gather.3.cloned.1.call-update
  8.7 0.0 all-reduce.3.cloned.1.call-start
  8.7 86.1 %all-gather.5.cloned.1.call-done = bf16[3584,224]{1,0:T(8,128)(2,1)} async-done(((bf16[112,224]{1,0:T(8,128)(2,1)}), bf16[3584,224]{1,0:T(8,128)(2,1)}) %all-gather.5.cloned.1.call-update) | async-done | bytes 1605648 | tf_op jit(solution)/shard_map/all_gather | solution.py:25
  94.8 59.2 %all-gather.3.cloned.1.call-done = bf16[1024,3584]{0,1:T(8,128)(2,1)} async-done(((bf16[1024,224]{0,1:T(8,128)(2,1)}), bf16[1024,3584]{0,1:T(8,128)(2,1)}) %all-gather.3.cloned.1.call-update) | async-done | bytes 7340048 | tf_op jit(solution)/shard_map/all_gather | solution.py:13
  154.0 5.6 %fusion.49 = f32[1024,224]{0,1:T(8,128)S(1)} fusion(bf16[1024,3584]{0,1:T(8,128)(2,1)} %all-gather.3.cloned.1.call-done, bf16[3584,224]{1,0:T(8,128)(2,1)} %all-gather.5.cloned.1.call-done), kind=kOutput, calls=%fused_computation.68 | convolution fusion | flops 1644167168 | bytes 9863168 | tf_op jit(solution)/shard_map/dot_general | solution.py:23
  159.6 1.2 convolution_bitcast_fusion.1
  160.8 4.0 %fusion.50 = f32[3584,224]{1,0:T(8,128)} fusion(bf16[1024,3584]{0,1:T(8,128)(2,1)S(1)} %copy-done.1, bf16[1024,224]{0,1:T(8,128)(2,1)S(1)} %copy-done.2), kind=kOutput, calls=%fused_computation.69 | convolution fusion | flops 1644167168 | bytes 11010048 | tf_op jit(solution)/shard_map/dot_general | solution.py:17
  164.8 1.3 fusion.1
  166.2 8.0 %while.1 = (s32[]{:T(128)}, f32[512,512]{1,0:T(8,128)S(1)}, s32[4,2]{0,1:T(2,128)S(1)}, f32[4,128,128]{2,1,0:T(8,128)S(1)}, s32[]{:T(128)}) while((s32[]{:T(128)}, f32[512,512]{1,0:T(8,128)S(1)}, s32[4,2]{0,1:T(2,128)S(1)}, f32[4,128,128]{2,1,0:T(8,128)S(1)}, s32[]{:T(128)}) %tuple.26), condition=%wide.while_cond, body=%wide.while_body.sunk | while | flops 2 | bytes 131189 | solution.py:9
  166.2 0.1 constant_dynamic-slice_fusion.2
  166.3 0.6 fusion.67
  166.9 1.3 bitcast_dynamic-update-slice_fusion.2
  168.2 0.1 constant_dynamic-slice_fusion.2
  168.3 0.6 fusion.67
  168.9 1.3 bitcast_dynamic-update-slice_fusion.2
  170.2 0.1 constant_dynamic-slice_fusion.2
  170.3 0.6 fusion.67
  170.9 1.3 bitcast_dynamic-update-slice_fusion.2
  172.2 0.1 constant_dynamic-slice_fusion.2
  172.3 0.6 fusion.67
  172.9 1.3 bitcast_dynamic-update-slice_fusion.2
  174.2 39.3 %custom-call.5 = f32[4,128,128]{1,2,0:T(8,128)S(1)} custom-call(f32[4,128,128]{2,1,0:T(8,128)S(1)} %get-tuple-element.9), custom_call_target="InvertDiagBlocksLowerTriangular" | custom-call | tf_op jit(solution)/shard_map/triangular_solve | solution.py:9
  213.5 120.8 %all-reduce.3.cloned.1.call-done = (f32[512,224]{0,1:T(8,128)}, f32[3584,224]{1,0:T(8,128)}) async-done(((f32[512,224]{0,1:T(8,128)}, f32[3584,224]{1,0:T(8,128)}), (f32[512,224]{0,1:T(8,128)}, f32[3584,224]{1,0:T(8,128)})) %all-reduce.3.cloned.1.call-update) | async-done | bytes 3670032 | tf_op jit(solution)/shard_map/psum | solution.py:32
  334.3 1.1 fusion.30
  335.5 1.2 convolution_subtract_fusion.1
  336.6 0.2 fusion.35
  336.9 1.3 convolution_subtract_fusion.3
  338.1 0.3 fusion.37
  338.4 1.4 convolution_subtract_fusion.5
  339.8 0.2 fusion.39
  340.0 0.3 fusion.46
  340.3 0.3 convolution_subtract_fusion
  340.5 0.3 fusion.47
  340.8 0.3 convolution_subtract_fusion.2
  341.2 0.3 fusion.48
  341.5 0.5 convolution_subtract_fusion.4
  341.9 0.3 convolution_convert_fusion
  342.2 0.5 fusion
  342.7 1.3 copy.10
  344.0 11.5 %all-to-all-start = ((f32[16,64,224]{2,1,0:T(8,128)}), f32[16,64,224]{2,1,0:T(8,128)S(1)}, u32[]{:S(2)}, u32[]{:S(2)}) async-start(f32[16,64,224]{2,1,0:T(8,128)} %bitcast.6), calls=%async_computation | async-start | bytes 2097152 | tf_op jit(solution)/shard_map/all_to_all | solution.py:35
  355.5 1.6 dynamic-slice_multiply_fusion
  357.1 26.4 %all-to-all-done = f32[16,64,224]{2,1,0:T(8,128)S(1)} async-done(((f32[16,64,224]{2,1,0:T(8,128)}), f32[16,64,224]{2,1,0:T(8,128)S(1)}, u32[]{:S(2)}, u32[]{:S(2)}) %all-to-all-start) | async-done | bytes 917536 | tf_op jit(solution)/shard_map/all_to_all | solution.py:35
  383.5 0.6 copy.11
  384.1 0.6 all_to_all.17
  384.7 1.1 broadcast_divide_fusion
  (13 shorter events, 0.1 us)
Async XLA Ops:
  7.2 152.4 %copy-start = (bf16[1024,512]{1,0:T(8,128)(2,1)S(1)}, bf16[1024,512]{1,0:T(8,128)(2,1)}, u32[]{:S(2)}) copy-start(bf16[1024,512]{1,0:T(8,128)(2,1)} %param.8) | copy-start | bytes 3145732
  7.2 87.6 %all-gather.5.cloned.1.call-start = ((), (), s32[]{:S(2)}) async-start(), calls=%async_computation.2 | async-start | bytes 1892352 | tf_op jit(solution)/shard_map/all_gather | solution.py:25
  7.9 146.0 %all-gather.3.cloned.1.call-start = ((), (), s32[]{:S(2)}) async-start(), calls=%async_computation.1 | async-start | bytes 7798784 | tf_op jit(solution)/shard_map/all_gather | solution.py:13
  8.7 152.1 %copy-start.2 = (bf16[1024,224]{0,1:T(8,128)(2,1)S(1)}, bf16[1024,224]{0,1:T(8,128)(2,1)}, u32[]{:S(2)}) copy-start(bf16[1024,224]{0,1:T(8,128)(2,1)} %param.7) | copy-start | bytes 1376260
  8.7 325.6 %all-reduce.3.cloned.1.call-start = ((), (), s32[]{:S(2)}) async-start(), calls=%async_computation.3 | async-start | bytes 8257536 | tf_op jit(solution)/shard_map/psum | solution.py:32
  154.0 6.8 %copy-start.1 = (bf16[1024,3584]{0,1:T(8,128)(2,1)S(1)}, bf16[1024,3584]{0,1:T(8,128)(2,1)}, u32[]{:S(2)}) copy-start(bf16[1024,3584]{0,1:T(8,128)(2,1)} %all-gather.3.cloned.1.call-done) | copy-start | bytes 22020100
  341.9 13.6 %copy-start.3 = (s32[64]{0:T(128)S(1)}, s32[64]{0:T(128)}, u32[]{:S(2)}) copy-start(s32[64]{0:T(128)} %param.11) | copy-start | bytes 772
  344.0 39.5 %all-to-all-start = ((f32[16,64,224]{2,1,0:T(8,128)}), f32[16,64,224]{2,1,0:T(8,128)S(1)}, u32[]{:S(2)}, u32[]{:S(2)}) async-start(f32[16,64,224]{2,1,0:T(8,128)} %bitcast.6), calls=%async_computation | async-start | bytes 2097152 | tf_op jit(solution)/shard_map/all_to_all | solution.py:35
Sparse Core Ops, SparseCore 0:
  11.1 83.6 all-gather.4
  96.9 57.0 all-gather.2
  164.9 169.3 all-reduce.2
where the time goes:
time: 393 us; the launch traced here: 392 us
  waiting for transfers between devices  294 us (75%)
  other arithmetic  43.3 us (11%)
  matrix products  19.1 us (5%)
  between operations  14 us (4%)
  starting transfers between devices  11.6 us (3%)
  local copies, waits for them, and re-layouts  10.5 us (3%)
    psum x1, waiting for transfers between devices, shards(): moments = lax.psum(partial_value, 'dp')  121 us
    all_gather x1, waiting for transfers between devices, shards(): lax.all_gather(proj_weight, 'dp', axis=0, tiled=True)  86.1 us
    all_gather x1, waiting for transfers between devices, shards(): grad_full = lax.all_gather(grad_out, 'col', axis=1, tiled=True)  59.2 us
    another operation x3, other arithmetic, solve_gram(): lax.linalg.triangular_solve(factor, inner, left_side=True, lower=True, tr...  40.7 us
    all_to_all x1, waiting for transfers between devices, shards(): lax.all_to_all(pooled, 'col', split_axis=0, concat_axis=1, tiled=True)  26.4 us
    all_to_all x1, starting transfers between devices, shards(): lax.all_to_all(pooled, 'col', split_axis=0, concat_axis=1, tiled=True)  11.5 us
    another operation x12, local copies, waits for them, and re-layouts  7.92 us
  transfers between devices with their start and end apart: 4, of which 4 were waited for; matrix products, arithmetic and copies ran while one was open for 13% of the time, Pallas kernels for 0%

commit v1 on v0

--- a/solution.py
+++ b/solution.py
@@ -29,7 +29,9 @@
     partial_value = lax.dot_general(
         confounders, dense_b, (((0,), (0,)), ((), ())), preferred_element_type=jnp.float32
     )
-    moments = lax.psum(partial_value, "dp")
+    moments = partial_value
+    for hop in (1, 2, 4, 8, 16):
+        moments = moments + lax.ppermute(moments, "dp", [(dev, dev ^ hop) for dev in range(32)])
     coef_b = solve_gram(gram_factor, moments).astype(jnp.bfloat16)
     pooled = dense_grad - jnp.dot(confounders, coef_b, preferred_element_type=jnp.float32)
     doc_grad = lax.all_to_all(pooled, "col", split_axis=0, concat_axis=1, tiled=True)

time: 393 us -> 450 us (1.15)
  waiting for transfers between devices: 294 us -> 324 us
  starting transfers between devices: 11.6 us -> 29.5 us
  other arithmetic: 43.3 us -> 49.1 us
    ppermute x0 -> x5, waiting for transfers between devices: none -> 35.4 us  [shards(): lax.ppermute(moments, 'dp', [(dev, dev ^ hop) for dev in range(32)])]
    all_to_all x1, waiting for transfers between devices: 26.4 us -> 0.01 us  [shards(): lax.all_to_all(pooled, 'col', split_axis=0, concat_axis=1, tiled=True)]
    psum x1, waiting for transfers between devices: 121 us -> 142 us  [shards(): summed_all = lax.psum(full_term, 'dp')]
    ppermute x0 -> x5, starting transfers between devices: none -> 20.1 us  [shards(): lax.ppermute(moments, 'dp', [(dev, dev ^ hop) for dev in range(32)])]
  transfers between devices with their start and end apart: 4 -> 9, of which waited for: 4 -> 7; matrix products, arithmetic and copies ran while one was open for 13% -> 15% of each run, Pallas kernels for 0% -> 0%
where the time goes in v1:
time: 450 us; the launch traced here: 447 us
  waiting for transfers between devices  324 us (72%)
  other arithmetic  49.1 us (11%)
  starting transfers between devices  29.5 us (7%)
  matrix products  17.6 us (4%)
  between operations  14 us (3%)
  local copies, waits for them, and re-layouts  12.9 us (3%)
    psum x1, waiting for transfers between devices, shards(): summed_all = lax.psum(full_term, 'dp')  142 us
    all_gather x1, waiting for transfers between devices, shards(): lax.all_gather(proj_weight, 'dp', axis=0, tiled=True)  86.1 us
    all_gather x1, waiting for transfers between devices, shards(): grad_full = lax.all_gather(grad_out, 'col', axis=1, tiled=True)  59.2 us
    another operation x3, other arithmetic, solve_gram(): lax.linalg.triangular_solve(factor, inner, left_side=True, lower=True, tr...  42.1 us
    ppermute x5, waiting for transfers between devices, shards(): lax.ppermute(moments, 'dp', [(dev, dev ^ hop) for dev in range(32)])  35.4 us
    ppermute x5, starting transfers between devices, shards(): lax.ppermute(moments, 'dp', [(dev, dev ^ hop) for dev in range(32)])  20.1 us
    another operation x12, local copies, waits for them, and re-layouts  10.3 us
    all_to_all x1, starting transfers between devices, shards(): lax.all_to_all(pooled, 'col', split_axis=0, concat_axis=1, tiled=True)  9.27 us
  transfers between devices with their start and end apart: 9, of which 7 were waited for; matrix products, arithmetic and copies ran while one was open for 15% of the time, Pallas kernels for 0%

profile of v1, /device:TPU:1, one launch (start us, length us, event | category | flops | bytes accessed | tf_op | source)
XLA Modules:
  0.0 447.4 jit_solution(7003875107565673772)
XLA Ops:
  7.2 0.7 all-gather.5.cloned.1.call-update
  8.0 0.7 all-gather.3.cloned.1.call-update
  8.7 86.1 %all-gather.5.cloned.1.call-done = bf16[3584,224]{1,0:T(8,128)(2,1)} async-done(((bf16[112,224]{1,0:T(8,128)(2,1)}), bf16[3584,224]{1,0:T(8,128)(2,1)}) %all-gather.5.cloned.1.call-update) | async-done | bytes 1605648 | tf_op jit(solution)/shard_map/all_gather | solution.py:25
  94.8 59.2 %all-gather.3.cloned.1.call-done = bf16[1024,3584]{0,1:T(8,128)(2,1)} async-done(((bf16[1024,224]{0,1:T(8,128)(2,1)}), bf16[1024,3584]{0,1:T(8,128)(2,1)}) %all-gather.3.cloned.1.call-update) | async-done | bytes 7340048 | tf_op jit(solution)/shard_map/all_gather | solution.py:13
  154.0 5.4 %fusion.52 = f32[1024,224]{0,1:T(8,128)S(1)} fusion(bf16[1024,3584]{0,1:T(8,128)(2,1)} %all-gather.3.cloned.1.call-done, bf16[3584,224]{1,0:T(8,128)(2,1)} %all-gather.5.cloned.1.call-done), kind=kOutput, calls=%fused_computation.71 | convolution fusion | flops 1644167168 | bytes 9863168 | tf_op jit(solution)/shard_map/dot_general | solution.py:23
  159.4 0.4 convolution_bitcast_fusion.1
  159.8 3.1 collective-permute-start
  162.9 10.6 %collective-permute-done = f32[512,224]{0,1:T(8,128)S(1)} collective-permute-done((f32[512,224]{0,1:T(8,128)S(1)}, f32[512,224]{0,1:T(8,128)S(1)}, u32[]{:S(2)}, u32[]{:S(2)}) %collective-permute-start) | collective-permute-done | bytes 458784 | tf_op jit(solution)/shard_map/ppermute | solution.py:34
  173.6 4.6 %collective-permute-start.1 = (f32[512,224]{0,1:T(8,128)S(1)}, f32[512,224]{0,1:T(8,128)S(1)}, u32[]{:S(2)}, u32[]{:S(2)}) collective-permute-start(f32[512,224]{0,1:T(8,128)S(1)} %add.24), channel_id=1, source_target_pairs={{0,32},{16,48},{32,0},{48,16},{64,96},{80,112},{96,64},{112,80},{1... | collective-permute-start | bytes 1376264 | tf_op jit(solution)/shard_map/ppermute | solution.py:34
  178.2 9.7 %collective-permute-done.1 = f32[512,224]{0,1:T(8,128)S(1)} collective-permute-done((f32[512,224]{0,1:T(8,128)S(1)}, f32[512,224]{0,1:T(8,128)S(1)}, u32[]{:S(2)}, u32[]{:S(2)}) %collective-permute-start.1) | collective-permute-done | bytes 458784 | tf_op jit(solution)/shard_map/ppermute | solution.py:34
  188.0 3.1 collective-permute-start.2
  191.2 1.3 fusion.1
  192.5 7.6 %collective-permute-done.2 = f32[512,224]{0,1:T(8,128)} collective-permute-done((f32[512,224]{0,1:T(8,128)S(1)}, f32[512,224]{0,1:T(8,128)}, u32[]{:S(2)}, u32[]{:S(2)}) %collective-permute-start.2) | collective-permute-done | bytes 458784 | tf_op jit(solution)/shard_map/ppermute | solution.py:34
  200.1 1.2 add.26
  201.3 4.0 collective-permute-start.3
  205.4 10.4 %while.1 = (s32[]{:T(128)}, f32[512,512]{1,0:T(8,128)S(1)}, s32[4,2]{0,1:T(2,128)S(1)}, f32[4,128,128]{2,1,0:T(8,128)}, s32[]{:T(128)}) while((s32[]{:T(128)}, f32[512,512]{1,0:T(8,128)S(1)}, s32[4,2]{0,1:T(2,128)S(1)}, f32[4,128,128]{2,1,0:T(8,128)}, s32[]{:T(128)}) %tuple.26), condition=%wide.while_cond, body=%wide.while_body.sunk | while | flops 2 | bytes 132205 | solution.py:9
  205.5 0.5 fusion.67
  206.0 2.0 bitcast_dynamic-update-slice_fusion.2
  208.1 0.5 fusion.67
  208.6 2.0 bitcast_dynamic-update-slice_fusion.2
  210.7 0.5 fusion.67
  211.2 2.0 bitcast_dynamic-update-slice_fusion.2
  213.3 0.5 fusion.67
  213.8 2.0 bitcast_dynamic-update-slice_fusion.2
  215.8 40.8 %custom-call.5 = f32[4,128,128]{1,2,0:T(8,128)} custom-call(f32[4,128,128]{2,1,0:T(8,128)} %get-tuple-element.9), custom_call_target="InvertDiagBlocksLowerTriangular" | custom-call | tf_op jit(solution)/shard_map/triangular_solve | solution.py:9
  256.5 1.8 add.27
  258.4 5.3 %collective-permute-start.4 = (f32[512,224]{0,1:T(8,128)}, f32[512,224]{0,1:T(8,128)}, u32[]{:S(2)}, u32[]{:S(2)}) collective-permute-start(f32[512,224]{0,1:T(8,128)} %add.27), channel_id=1, source_target_pairs={{0,256},{16,272},{32,288},{48,304},{64,320},{80,336},{96,352},{112... | collective-permute-start | bytes 1376264 | tf_op jit(solution)/shard_map/ppermute | solution.py:34
  263.7 7.1 %fusion.53 = f32[3584,224]{1,0:T(8,128)} fusion(bf16[1024,3584]{0,1:T(8,128)(2,1)} %all-gather.3.cloned.1.call-done, bf16[1024,224]{0,1:T(8,128)(2,1)} %param.7), kind=kOutput, calls=%fused_computation.72 | convolution fusion | flops 1644167168 | bytes 11010048 | tf_op jit(solution)/shard_map/dot_general | solution.py:17
  270.8 7.5 %collective-permute-done.4 = f32[512,224]{0,1:T(8,128)} collective-permute-done((f32[512,224]{0,1:T(8,128)}, f32[512,224]{0,1:T(8,128)}, u32[]{:S(2)}, u32[]{:S(2)}) %collective-permute-start.4) | collective-permute-done | bytes 458784 | tf_op jit(solution)/shard_map/ppermute | solution.py:34
  278.3 1.2 add.28
  279.8 0.3 fusion.38
  280.3 0.4 fusion.14
  280.9 0.5 fusion.3
  281.7 0.3 fusion.49
  281.9 0.2 convolution_subtract_fusion
  282.2 0.3 fusion.50
  282.5 0.4 convolution_subtract_fusion.1
  282.8 0.3 fusion.51
  283.1 0.5 convolution_subtract_fusion.2
  283.6 0.3 convolution_convert_fusion
  283.8 0.5 fusion
  284.3 1.3 copy.10
  285.6 9.3 %all-to-all-start = ((f32[16,64,224]{2,1,0:T(8,128)}), f32[16,64,224]{2,1,0:T(8,128)S(1)}, u32[]{:S(2)}, u32[]{:S(2)}) async-start(f32[16,64,224]{2,1,0:T(8,128)} %bitcast.6), calls=%async_computation | async-start | bytes 2097152 | tf_op jit(solution)/shard_map/all_to_all | solution.py:37
  294.9 142.1 %all-reduce.2.cloned.1.call-done = f32[3584,224]{1,0:T(8,128)} async-done(((f32[3584,224]{1,0:T(8,128)}), f32[3584,224]{1,0:T(8,128)}) %all-reduce.2.cloned.1.call-update) | async-done | bytes 3211280 | tf_op jit(solution)/shard_map/psum | solution.py:20
  437.0 1.6 dynamic-slice_multiply_fusion
  438.6 0.6 copy.11
  439.2 0.6 all_to_all.17
  439.8 1.1 broadcast_divide_fusion
  (28 shorter events, 1.6 us)
Async XLA Ops:
  7.2 152.3 %copy-start = (bf16[1024,512]{1,0:T(8,128)(2,1)S(1)}, bf16[1024,512]{1,0:T(8,128)(2,1)}, u32[]{:S(2)}) copy-start(bf16[1024,512]{1,0:T(8,128)(2,1)} %param.8) | copy-start | bytes 3145732
  7.2 87.6 %all-gather.5.cloned.1.call-start = ((), (), s32[]{:S(2)}) async-start(), calls=%async_computation.2 | async-start | bytes 1892352 | tf_op jit(solution)/shard_map/all_gather | solution.py:25
  7.9 146.0 %all-gather.3.cloned.1.call-start = ((), (), s32[]{:S(2)}) async-start(), calls=%async_computation.1 | async-start | bytes 7798784 | tf_op jit(solution)/shard_map/all_gather | solution.py:13
  8.7 428.3 %all-reduce.2.cloned.1.call-start = ((), (), s32[]{:S(2)}) async-start(), calls=%async_computation.3 | async-start | bytes 7340032 | tf_op jit(solution)/shard_map/psum | solution.py:20
  159.8 13.7 %collective-permute-start = (f32[512,224]{0,1:T(8,128)S(1)}, f32[512,224]{0,1:T(8,128)S(1)}, u32[]{:S(2)}, u32[]{:S(2)}) collective-permute-start(f32[512,224]{0,1:T(8,128)S(1)} %convolution_bitcast_fusion.1), channel_id=1, source_target_pairs={{0,16},{16,0},{32,48},{48,32},{64,80},{80,64},{96,112},{112,96},{1... | collective-permute-start | bytes 1376264 | tf_op jit(solution)/shard_map/ppermute | solution.py:34
  173.6 14.3 %collective-permute-start.1 = (f32[512,224]{0,1:T(8,128)S(1)}, f32[512,224]{0,1:T(8,128)S(1)}, u32[]{:S(2)}, u32[]{:S(2)}) collective-permute-start(f32[512,224]{0,1:T(8,128)S(1)} %add.24), channel_id=1, source_target_pairs={{0,32},{16,48},{32,0},{48,16},{64,96},{80,112},{96,64},{112,80},{1... | collective-permute-start | bytes 1376264 | tf_op jit(solution)/shard_map/ppermute | solution.py:34
  188.0 4.5 %copy-start.1 = (f32[512,224]{0,1:T(8,128)}, f32[512,224]{0,1:T(8,128)S(1)}, u32[]{:S(2)}) copy-start(f32[512,224]{0,1:T(8,128)S(1)} %add.25) | copy-start | bytes 1376260
  188.0 12.1 %collective-permute-start.2 = (f32[512,224]{0,1:T(8,128)S(1)}, f32[512,224]{0,1:T(8,128)}, u32[]{:S(2)}, u32[]{:S(2)}) collective-permute-start(f32[512,224]{0,1:T(8,128)S(1)} %add.25), channel_id=1, source_target_pairs={{0,64},{16,80},{32,96},{48,112},{64,0},{80,16},{96,32},{112,48},{1... | collective-permute-start | bytes 1376264 | tf_op jit(solution)/shard_map/ppermute | solution.py:34
  201.3 55.2 %collective-permute-start.3 = (f32[512,224]{0,1:T(8,128)S(1)}, f32[512,224]{0,1:T(8,128)}, u32[]{:S(2)}, u32[]{:S(2)}) collective-permute-start(f32[512,224]{0,1:T(8,128)S(1)} %add.26), channel_id=1, source_target_pairs={{0,128},{16,144},{32,160},{48,176},{64,192},{80,208},{96,224},{112... | collective-permute-start | bytes 1376264 | tf_op jit(solution)/shard_map/ppermute | solution.py:34
  258.4 19.9 %collective-permute-start.4 = (f32[512,224]{0,1:T(8,128)}, f32[512,224]{0,1:T(8,128)}, u32[]{:S(2)}, u32[]{:S(2)}) collective-permute-start(f32[512,224]{0,1:T(8,128)} %add.27), channel_id=1, source_target_pairs={{0,256},{16,272},{32,288},{48,304},{64,320},{80,336},{96,352},{112... | collective-permute-start | bytes 1376264 | tf_op jit(solution)/shard_map/ppermute | solution.py:34
  270.8 8.8 %copy-start.2 = (f32[4,128,128]{1,2,0:T(8,128)S(1)}, f32[4,128,128]{1,2,0:T(8,128)}, u32[]{:S(2)}) copy-start(f32[4,128,128]{1,2,0:T(8,128)} %custom-call.5) | copy-start | bytes 786436
  283.6 11.4 %copy-start.3 = (s32[64]{0:T(128)S(1)}, s32[64]{0:T(128)}, u32[]{:S(2)}) copy-start(s32[64]{0:T(128)} %param.11) | copy-start | bytes 772
  285.6 152.9 %all-to-all-start = ((f32[16,64,224]{2,1,0:T(8,128)}), f32[16,64,224]{2,1,0:T(8,128)S(1)}, u32[]{:S(2)}, u32[]{:S(2)}) async-start(f32[16,64,224]{2,1,0:T(8,128)} %bitcast.6), calls=%async_computation | async-start | bytes 2097152 | tf_op jit(solution)/shard_map/all_to_all | solution.py:37
Sparse Core Ops, SparseCore 0:
  11.1 83.6 all-gather.4
  96.9 57.0 all-gather.2
  270.9 166.0 all-reduce.1
